TPU v7x, 128 devices: a whole 4x4x4 slice. The times are simulated.
128 devices in a mesh: dp: 32 (over y, z, core), bn: 4 (over x).
Axes of the slice: x: 4, y: 4, z: 4, core: 2. Of those that a mesh axis runs over, the one named last changes fastest.
Arguments:
- key_feats: bfloat16 [1024, 12, 16, 2048], P(('dp', 'bn')), may hold values from -22 to 22
- clip_starts: int32 [1024], P(('dp', 'bn')), may hold values from 0 to 4
- shuffle: int32 [4, 32], P('bn'), may hold values from 0 to 31, each once within a row
- query_feats: bfloat16 [1024, 2048], P(('dp', 'bn')), may hold values from -6 to 6
- conv_time: bfloat16 [3, 2048, 512], replicated, may hold values from -0.078125 to 0.078125
- conv_space: bfloat16 [9, 512, 512], replicated, may hold values from -0.09375 to 0.09375
- conv_expand: bfloat16 [512, 2048], replicated, may hold values from -0.25 to 0.25
- gain_one: float32 [512], replicated, may hold values from 0.25 to 1.75
- shift_one: float32 [512], replicated, may hold values from -3 to 3
- gain_two: float32 [512], replicated, may hold values from 0.25 to 1.75
- shift_two: float32 [512], replicated, may hold values from -3 to 3
- gain_three: float32 [2048], replicated, may hold values from 0.25 to 1.75
- shift_three: float32 [2048], replicated, may hold values from -3 to 3
- w_key: bfloat16 [2048, 128], replicated, may hold values from -0.125 to 0.125
- w_query: bfloat16 [2048, 128], replicated, may hold values from -0.125 to 0.125
- queue: bfloat16 [16384, 128], replicated, may hold values from -6 to 6
Outputs:
- keys: bfloat16 [1024, 128], P(('dp', 'bn'))
- query_grad: float32 [2048, 128], replicated
Inputs may be any that keep to these rules, and one draw needn't show every extreme that they name: `shuffle`: each row is a permutation of 0 to 31.
All inputs are finite; a program needn't handle non-finite values.
Results may differ from a plain program's by a relative error of at most 0.0061.
Values may be sent and summed in bfloat16 or wider, within the bound.
A program may use at most 128 MiB of HBM per device.

v0:
```python
import jax
import jax.numpy as jnp
from jax import lax
from jax.sharding import PartitionSpec as P

FRAMES = 8
SIDE = 4
SHARPNESS_DIVISOR = 0.2
EPSILON = 1e-05


def pick_frames(features, starts):

    def single(clip_feats, first_frame):
        return lax.dynamic_slice_in_dim(clip_feats, first_frame, FRAMES, 0)

    return jax.vmap(single)(features, starts)


def time_conv(values, weights):
    padded = jnp.pad(values, ((0, 0), (1, 1), (0, 0), (0, 0)))
    length = values.shape[1]
    summed = jnp.zeros(values.shape[:3] + (weights.shape[2],), jnp.float32)
    for offset in range(3):
        summed = summed + jnp.einsum(
            "afsc,cd->afsd",
            padded[:, offset : offset + length],
            weights[offset],
            preferred_element_type=jnp.float32,
        )
    return summed


def space_conv(values, weights):
    square_grid = values.reshape(values.shape[0], values.shape[1], SIDE, SIDE, values.shape[3])
    padded = jnp.pad(square_grid, ((0, 0), (0, 0), (1, 1), (1, 1), (0, 0)))
    summed = jnp.zeros(
        (values.shape[0], values.shape[1], SIDE, SIDE, weights.shape[2]), jnp.float32
    )
    for row_shift in range(3):
        for col_shift in range(3):
            window = padded[:, :, row_shift : row_shift + SIDE, col_shift : col_shift + SIDE]
            summed = summed + jnp.einsum(
                "afhwc,cd->afhwd",
                window,
                weights[3 * row_shift + col_shift],
                preferred_element_type=jnp.float32,
            )
    return summed.reshape(values.shape[0], values.shape[1], SIDE * SIDE, weights.shape[2])


def batch_norm(values, total_sum, squares, row_count, gain_row, shift_row):
    center = total_sum / row_count
    spread = squares / row_count - center * center
    return (values - center) * (gain_row * lax.rsqrt(spread + EPSILON)) + shift_row


def encode(values, params, moments, row_count):
    (
        conv_time,
        conv_space,
        conv_expand,
        gain_one,
        shift_one,
        gain_two,
        shift_two,
        gain_three,
        shift_three,
        w_key,
    ) = params
    first_out = time_conv(values, conv_time)
    total_sum, squares = moments(first_out)
    act_one = jnp.maximum(
        batch_norm(first_out, total_sum, squares, row_count, gain_one, shift_one), 0.0
    ).astype(jnp.bfloat16)
    second = space_conv(act_one, conv_space)
    total_sum, squares = moments(second)
    act_two = jnp.maximum(
        batch_norm(second, total_sum, squares, row_count, gain_two, shift_two), 0.0
    ).astype(jnp.bfloat16)
    third_out = jnp.einsum(
        "afsc,cd->afsd", act_two, conv_expand, preferred_element_type=jnp.float32
    )
    total_sum, squares = moments(third_out)
    merged = jnp.maximum(
        batch_norm(third_out, total_sum, squares, row_count, gain_three, shift_three)
        + values.astype(jnp.float32),
        0.0,
    )
    pooled = jnp.mean(merged, axis=(1, 2)).astype(jnp.bfloat16)
    projected = jnp.dot(pooled, w_key, preferred_element_type=jnp.float32)
    return (
        projected * lax.rsqrt(jnp.sum(projected * projected, axis=-1, keepdims=True) + 1e-06)
    ).astype(jnp.bfloat16)


def query_terms(query_feats, own_keys, w_query, queue):
    projected = jnp.dot(query_feats, w_query, preferred_element_type=jnp.float32)
    length = jnp.sqrt(jnp.sum(projected * projected, axis=-1, keepdims=True) + 1e-06)
    anchor_direction = projected / length
    queue_wide = queue.astype(jnp.float32)
    memory_bank_directions = (
        queue_wide * lax.rsqrt(jnp.sum(queue_wide * queue_wide, axis=-1, keepdims=True) + 1e-06)
    ).astype(jnp.bfloat16)
    collected_encodings = own_keys.astype(jnp.float32)
    matching_scores = jnp.sum(anchor_direction * collected_encodings, axis=-1) / SHARPNESS_DIVISOR
    distractor_scores = (
        jnp.einsum(
            "nf,ef->ne",
            anchor_direction.astype(jnp.bfloat16),
            memory_bank_directions,
            preferred_element_type=jnp.float32,
        )
        / SHARPNESS_DIVISOR
    )
    partition = jnp.exp(matching_scores) + jnp.sum(jnp.exp(distractor_scores), axis=-1)
    log_total = jnp.log(partition)
    weight_pos = jnp.exp(matching_scores - log_total)
    weight_neg = jnp.exp(distractor_scores - log_total[:, None]).astype(jnp.bfloat16)
    retrieved_samples = (
        jnp.dot(weight_neg, memory_bank_directions, preferred_element_type=jnp.float32)
        + (weight_pos - 1.0)[:, None] * collected_encodings
    )
    anchor_loss_derivative = retrieved_samples / SHARPNESS_DIVISOR
    radial = jnp.sum(anchor_direction * anchor_loss_derivative, axis=-1, keepdims=True)
    return ((anchor_loss_derivative - radial * anchor_direction) / length).astype(jnp.bfloat16)


def local(
    key_feats,
    clip_starts,
    shuffle,
    query_feats,
    conv_time,
    conv_space,
    conv_expand,
    gain_one,
    shift_one,
    gain_two,
    shift_two,
    gain_three,
    shift_three,
    w_key,
    w_query,
    queue,
):
    params = (
        conv_time,
        conv_space,
        conv_expand,
        gain_one,
        shift_one,
        gain_two,
        shift_two,
        gain_three,
        shift_three,
        w_key,
    )
    chosen = pick_frames(key_feats, clip_starts)
    peer_count = lax.axis_size("dp")
    groups = lax.axis_size("bn")
    target = shuffle[0, lax.axis_index("dp")]
    row_count = groups * chosen.shape[0] * chosen.shape[1] * chosen.shape[2]
    slot = (jnp.arange(peer_count, dtype=jnp.int32) == target).astype(jnp.float32)

    def group_moments(values):
        sums = jnp.stack(
            [jnp.sum(values, axis=(0, 1, 2)), jnp.sum(values * values, axis=(0, 1, 2))]
        )
        table = lax.psum(slot[:, None, None] * sums[None], ("dp", "bn"))
        own = lax.dynamic_index_in_dim(table, target, 0, keepdims=False)
        return (own[0], own[1])

    own_keys = encode(chosen, params, group_moments, row_count)
    grad_proj = query_terms(query_feats, own_keys, w_query, queue)
    grad_part = jnp.einsum("nc,ne->ce", query_feats, grad_proj, preferred_element_type=jnp.float32)
    query_grad = lax.psum(grad_part, ("dp", "bn"))
    return (own_keys, query_grad)


def solution(mesh):
    placed = (
        P(("dp", "bn"), None, None, None),
        P(("dp", "bn")),
        P("bn", None),
        P(("dp", "bn"), None),
        P(),
        P(),
        P(),
        P(),
        P(),
        P(),
        P(),
        P(),
        P(),
        P(),
        P(),
        P(),
    )
    return jax.shard_map(
        local, mesh=mesh, in_specs=placed, out_specs=(P(("dp", "bn"), None), P()), check_vma=False
    )
```

profile of v0, /device:TPU:1, one launch (start us, length us, event | category | flops | bytes accessed | tf_op | source)
XLA Modules:
  0.0 665.7 jit_solution(5777000886677736291)
XLA Ops:
  7.2 6.7 %copy.18 = bf16[8,12,16,2048]{3,2,0,1:T(8,128)(2,1)} copy(bf16[8,12,16,2048]{3,2,1,0:T(8,128)(2,1)} %param.16) | data formatting | bytes 12582912 | tf_op args[0]
  14.0 5.6 gather_fusion
  19.5 6.7 %fusion.6 = f32[8,8,16,512]{3,2,1,0:T(8,128)} fusion(bf16[8,8,16,2048]{3,2,1,0:T(8,128)(2,1)} %gather_fusion, bf16[3,2048,512]{2,1,0:T(8,128)(2,1)} %param.20), kind=kOutput, calls=%fused_computation.13 | convolution fusion | flops 2147483648 | bytes 8388608 | tf_op jit(solution)/shard_map/afsc,cd->afsd/dot_general | solution.py:25
  26.2 5.2 fusion.8
  32.7 7.7 %fusion.75 = (f32[512]{0:T(512)S(1)}, f32[512]{0:T(512)S(1)}, f32[8,8,16,512]{3,2,1,0:T(8,128)}) fusion(bf16[8,8,16,2048]{3,2,1,0:T(8,128)(2,1)} %gather_fusion, bf16[3,2048,512]{2,1,0:T(8,128)(2,1)} %param.20, f32[8,8,16,512]{3,2,1,0:T(8,128)} %fusion.8, f32[8,8,16,512]{3,2,1,0:T(8,128)} %fusion.6), kind=kOutput, calls=%fused_computation.113 | convolution fusion | flops 1881668608 | bytes 12587008 | tf_op jit(solution)/shard_map/afsc,cd->afsd/dot_general | solution.py:25
  40.4 0.8 broadcast_multiply_fusion.2
  43.2 143.4 %all-reduce.8.cloned.1.call-done = f32[32,2,512]{2,1,0:T(2,128)} async-done(((f32[32,2,512]{2,1,0:T(2,128)}), f32[32,2,512]{2,1,0:T(2,128)}) %all-reduce.8.cloned.1.call-update) | async-done | bytes 131088 | tf_op jit(solution)/shard_map/psum | solution.py:170
  186.6 0.8 dynamic-slice_multiply_fusion.5
  187.4 2.1 maximum_convert_fusion
  190.1 1.8 fusion.34
  191.9 1.7 fusion.36
  193.7 1.7 fusion.38
  195.4 0.7 fusion.40
  196.1 0.7 fusion.42
  196.9 0.7 fusion.44
  197.6 0.7 fusion.46
  198.3 0.7 fusion.48
  199.0 2.6 fusion.74
  201.6 0.8 broadcast_multiply_fusion.1
  202.7 3.9 fusion
  206.6 135.4 %all-reduce.10.cloned.1.call-done = f32[32,2,512]{2,1,0:T(2,128)} async-done(((f32[32,2,512]{2,1,0:T(2,128)}), f32[32,2,512]{2,1,0:T(2,128)}) %all-reduce.10.cloned.1.call-update) | async-done | bytes 131088 | tf_op jit(solution)/shard_map/psum | solution.py:170
  342.0 0.8 dynamic-slice_multiply_fusion.3
  342.9 8.0 %fusion.73 = (f32[2048]{0:T(1024)S(1)}, f32[2048]{0:T(1024)S(1)}, f32[8,8,16,2048]{3,2,1,0:T(8,128)}) fusion(bf16[512,2048]{1,0:T(8,128)(2,1)S(1)} %copy-done, f32[8,8,16,512]{3,1,2,0:T(8,128)} %bitcast.149, f32[512]{0:T(512)S(1)} %copy-done.12, f32[512]{0:T(512)S(1)} %rsqrt_multiply_fusion.1, f32[512]{0:T(512)S(1)} %bitcast.160), kind=kOutput, calls=%fused_computation.111 | convolution fusion | flops 2156392448 | bytes 12605440 | tf_op jit(solution)/shard_map/afsc,cd->afsd/dot_general | solution.py:81
  350.9 1.0 broadcast_multiply_fusion
  352.3 143.8 %all-reduce.12.cloned.1.call-done = f32[32,2,2048]{2,1,0:T(2,128)} async-done(((f32[32,2,2048]{2,1,0:T(2,128)}), f32[32,2,2048]{2,1,0:T(2,128)}) %all-reduce.12.cloned.1.call-update) | async-done | bytes 524304 | tf_op jit(solution)/shard_map/psum | solution.py:170
  496.1 0.8 dynamic-slice_multiply_fusion.1
  496.9 5.8 maximum_reduce_fusion
  503.1 2.5 exponential_reduce_fusion
  505.8 2.5 multiply_reduce_fusion.3
  508.3 1.4 convolution_bitcast_fusion
  509.7 147.0 %all-reduce.14.cloned.1.call-done = f32[2048,128]{0,1:T(8,128)} async-done(((f32[2048,128]{0,1:T(8,128)}), f32[2048,128]{0,1:T(8,128)}) %all-reduce.14.cloned.1.call-update) | async-done | bytes 1048592 | tf_op jit(solution)/shard_map/psum | solution.py:177
  656.7 2.5 copy.22
  (59 shorter events, 3.2 us)
Async XLA Ops:
  7.2 335.6 %copy-start = (bf16[512,2048]{1,0:T(8,128)(2,1)S(1)}, bf16[512,2048]{1,0:T(8,128)(2,1)}, u32[]{:S(2)}) copy-start(bf16[512,2048]{1,0:T(8,128)(2,1)} %param.22) | copy-start | bytes 6291460
  7.2 6.8 %copy-start.13 = (s32[8]{0:T(128)S(1)}, s32[8]{0:T(128)}, u32[]{:S(2)}) copy-start(s32[8]{0:T(128)} %param.17) | copy-start | bytes 100
  7.2 179.4 %all-reduce.8.cloned.1.call-start = ((), (), s32[]{:S(2)}) async-start(), calls=%async_computation | async-start | bytes 262144 | tf_op jit(solution)/shard_map/psum | solution.py:170
  19.5 6.7 %copy-start.2 = (bf16[8,8,16,2048]{3,2,1,0:T(8,128)(2,1)S(1)}, bf16[8,8,16,2048]{3,2,1,0:T(8,128)(2,1)}, u32[]{:S(2)}) copy-start(bf16[8,8,16,2048]{3,2,1,0:T(8,128)(2,1)} %gather_fusion) | copy-start | bytes 12582916
  26.2 5.2 copy-start.14
  32.7 154.6 %copy-start.8 = (f32[512]{0:T(512)S(1)}, f32[512]{0:T(512)}, u32[]{:S(2)}) copy-start(f32[512]{0:T(512)} %param.23) | copy-start | bytes 6148
  32.7 154.6 %copy-start.11 = (f32[512]{0:T(512)S(1)}, f32[512]{0:T(512)}, u32[]{:S(2)}) copy-start(f32[512]{0:T(512)} %param.24) | copy-start | bytes 6148
  41.2 300.9 %all-reduce.10.cloned.1.call-start = ((), (), s32[]{:S(2)}) async-start(), calls=%async_computation.1 | async-start | bytes 262144 | tf_op jit(solution)/shard_map/psum | solution.py:170
  187.3 8.1 %slice-start = ((s8[4718592]{0:T(1024)(128)(4,1)}), s8[4194304]{0:T(1024)(128)(4,1)S(1)}, s32[]{:S(2)}) async-start(s8[4718592]{0:T(1024)(128)(4,1)} %bitcast.147), calls=%async_computation.4 | async-start | bytes 8388608
  190.1 5.3 slice-start.1
  202.4 140.4 %copy-start.9 = (f32[512]{0:T(512)S(1)}, f32[512]{0:T(512)}, u32[]{:S(2)}) copy-start(f32[512]{0:T(512)} %param.25) | copy-start | bytes 6148
  202.4 140.4 %copy-start.12 = (f32[512]{0:T(512)S(1)}, f32[512]{0:T(512)}, u32[]{:S(2)}) copy-start(f32[512]{0:T(512)} %param.26) | copy-start | bytes 6148
  202.4 293.6 %all-reduce.12.cloned.1.call-start = ((), (), s32[]{:S(2)}) async-start(), calls=%async_computation.2 | async-start | bytes 1048576 | tf_op jit(solution)/shard_map/psum | solution.py:170
  342.8 9.2 %copy-start.3 = (bf16[2048,128]{1,0:T(8,128)(2,1)S(1)}, bf16[2048,128]{1,0:T(8,128)(2,1)}, u32[]{:S(2)}) copy-start(bf16[2048,128]{1,0:T(8,128)(2,1)} %param.30) | copy-start | bytes 1572868
  342.8 9.2 %copy-start.5 = (bf16[8,2048]{1,0:T(8,128)(2,1)S(1)}, bf16[8,2048]{1,0:T(8,128)(2,1)}, u32[]{:S(2)}) copy-start(bf16[8,2048]{1,0:T(8,128)(2,1)} %param.19) | copy-start | bytes 98308
  342.9 154.0 %copy-start.6 = (f32[2048]{0:T(1024)S(1)}, f32[2048]{0:T(1024)}, u32[]{:S(2)}) copy-start(f32[2048]{0:T(1024)} %param.27) | copy-start | bytes 24580
  342.9 154.0 %copy-start.7 = (f32[2048]{0:T(1024)S(1)}, f32[2048]{0:T(1024)}, u32[]{:S(2)}) copy-start(f32[2048]{0:T(1024)} %param.28) | copy-start | bytes 24580
  351.9 304.8 %all-reduce.14.cloned.1.call-start = ((), (), s32[]{:S(2)}) async-start(), calls=%async_computation.3 | async-start | bytes 2097152 | tf_op jit(solution)/shard_map/psum | solution.py:177
  496.9 5.9 copy-start.4
  496.9 6.2 copy-start.1
  505.8 2.5 copy-start.10
Sparse Core Ops, SparseCore 0:
  41.3 145.2 all-reduce.7
  202.5 139.4 all-reduce.9
  352.1 143.9 all-reduce.11
  509.8 146.8 all-reduce.13
where the time goes:
time: 666 us
  waiting for transfers between devices  570 us (86%)
  matrix products  45.9 us (7%)
  other arithmetic  17.6 us (3%)
  local copies, waits for them, and re-layouts  16.1 us (2%)
  between operations  16.1 us (2%)
    psum x3, waiting for transfers between devices, group_moments(): table = lax.psum(slot[:, None, None] * sums[None], ('dp', 'bn'))  423 us
    psum x1, waiting for transfers between devices, local(): query_grad = lax.psum(grad_part, ('dp', 'bn'))  147 us
    dot_general x3, matrix products, time_conv(): jnp.einsum('afsc,cd->afsd', padded[:, offset:offset + length], weights[of...  19.6 us
  transfers between devices with their start and end apart: 4, of which 4 were waited for; matrix products, arithmetic and copies ran while one was open for 1% of the time, Pallas kernels for 0%

commit v1 on v0

--- a/solution.py
+++ b/solution.py
@@ -174,7 +174,9 @@
     own_keys = encode(chosen, params, group_moments, row_count)
     grad_proj = query_terms(query_feats, own_keys, w_query, queue)
     grad_part = jnp.einsum("nc,ne->ce", query_feats, grad_proj, preferred_element_type=jnp.float32)
-    query_grad = lax.psum(grad_part, ("dp", "bn"))
+    query_grad = grad_part
+    for name in ("bn", "dp"):
+        query_grad = lax.psum(query_grad, name)
     return (own_keys, query_grad)
 
 

time: 666 us -> 674 us (1.012)
  waiting for transfers between devices: 570 us -> 577 us
    psum x1 -> x2, waiting for transfers between devices: 147 us -> 154 us  [local(): query_grad = lax.psum(query_grad, name)]
  transfers between devices with their start and end apart: 4 -> 5, of which waited for: 4 -> 5; matrix products, arithmetic and copies ran while one was open for 1% -> 1% of each run, Pallas kernels for 0% -> 0%
where the time goes in v1:
time: 674 us; the launch traced here: 673 us
  waiting for transfers between devices  577 us (86%)
  matrix products  45.9 us (7%)
  other arithmetic  17.6 us (3%)
  local copies, waits for them, and re-layouts  16.1 us (2%)
  between operations  16.1 us (2%)
    psum x3, waiting for transfers between devices, group_moments(): table = lax.psum(slot[:, None, None] * sums[None], ('dp', 'bn'))  423 us
    psum x2, waiting for transfers between devices, local(): query_grad = lax.psum(query_grad, name)  154 us
    dot_general x3, matrix products, time_conv(): jnp.einsum('afsc,cd->afsd', padded[:, offset:offset + length], weights[of...  19.6 us
  transfers between devices with their start and end apart: 5, of which 5 were waited for; matrix products, arithmetic and copies ran while one was open for 1% of the time, Pallas kernels for 0%

profile of v1, /device:TPU:1, one launch (start us, length us, event | category | flops | bytes accessed | tf_op | source)
XLA Modules:
  0.0 673.1 jit_solution(9411924003373527989)
XLA Ops:
  7.2 6.7 copy.18
  14.0 5.6 gather_fusion
  19.5 6.7 fusion.6
  26.2 5.2 fusion.8
  32.7 7.7 %fusion.75 = (f32[512]{0:T(512)S(1)}, f32[512]{0:T(512)S(1)}, f32[8,8,16,512]{3,2,1,0:T(8,128)}) fusion(bf16[8,8,16,2048]{3,2,1,0:T(8,128)(2,1)} %gather_fusion, bf16[3,2048,512]{2,1,0:T(8,128)(2,1)} %param.20, f32[8,8,16,512]{3,2,1,0:T(8,128)} %fusion.8, f32[8,8,16,512]{3,2,1,0:T(8,128)} %fusion.6), kind=kOutput, calls=%fused_computation.113 | convolution fusion | flops 1881668608 | bytes 12587008 | tf_op jit(solution)/shard_map/afsc,cd->afsd/dot_general | solution.py:25
  40.4 0.8 broadcast_multiply_fusion.2
  43.2 143.4 %all-reduce.9.cloned.1.call-done = f32[32,2,512]{2,1,0:T(2,128)} async-done(((f32[32,2,512]{2,1,0:T(2,128)}), f32[32,2,512]{2,1,0:T(2,128)}) %all-reduce.9.cloned.1.call-update) | async-done | bytes 131088 | tf_op jit(solution)/shard_map/psum | solution.py:170
  186.6 0.8 dynamic-slice_multiply_fusion.5
  187.4 2.1 maximum_convert_fusion
  190.1 1.8 fusion.34
  191.9 1.7 fusion.36
  193.7 1.7 fusion.38
  195.4 0.7 fusion.40
  196.1 0.7 fusion.42
  196.9 0.7 fusion.44
  198.3 0.7 fusion.48
  199.0 2.6 fusion.74
  201.6 0.8 broadcast_multiply_fusion.1
  202.7 3.9 fusion
  206.6 135.4 %all-reduce.11.cloned.1.call-done = f32[32,2,512]{2,1,0:T(2,128)} async-done(((f32[32,2,512]{2,1,0:T(2,128)}), f32[32,2,512]{2,1,0:T(2,128)}) %all-reduce.11.cloned.1.call-update) | async-done | bytes 131088 | tf_op jit(solution)/shard_map/psum | solution.py:170
  342.0 0.8 dynamic-slice_multiply_fusion.3
  342.9 8.0 %fusion.73 = (f32[2048]{0:T(1024)S(1)}, f32[2048]{0:T(1024)S(1)}, f32[8,8,16,2048]{3,2,1,0:T(8,128)}) fusion(bf16[512,2048]{1,0:T(8,128)(2,1)S(1)} %copy-done, f32[8,8,16,512]{3,1,2,0:T(8,128)} %bitcast.149, f32[512]{0:T(512)S(1)} %copy-done.12, f32[512]{0:T(512)S(1)} %rsqrt_multiply_fusion.1, f32[512]{0:T(512)S(1)} %bitcast.160), kind=kOutput, calls=%fused_computation.111 | convolution fusion | flops 2156392448 | bytes 12605440 | tf_op jit(solution)/shard_map/afsc,cd->afsd/dot_general | solution.py:81
  350.9 1.0 broadcast_multiply_fusion
  352.3 143.8 %all-reduce.13.cloned.1.call-done = f32[32,2,2048]{2,1,0:T(2,128)} async-done(((f32[32,2,2048]{2,1,0:T(2,128)}), f32[32,2,2048]{2,1,0:T(2,128)}) %all-reduce.13.cloned.1.call-update) | async-done | bytes 524304 | tf_op jit(solution)/shard_map/psum | solution.py:170
  496.1 0.8 dynamic-slice_multiply_fusion.1
  496.9 5.8 maximum_reduce_fusion
  503.1 2.5 exponential_reduce_fusion
  505.8 2.5 multiply_reduce_fusion.3
  508.3 1.4 convolution_bitcast_fusion
  509.7 42.8 %all-reduce.15.cloned.1.call-done = f32[2048,128]{0,1:T(8,128)} async-done(((f32[2048,128]{0,1:T(8,128)}), f32[2048,128]{0,1:T(8,128)}) %all-reduce.15.cloned.1.call-update) | async-done | bytes 1048592 | tf_op jit(solution)/shard_map/psum | solution.py:179
  552.5 111.5 %all-reduce.17.cloned.1.call-done = f32[2048,128]{0,1:T(8,128)} async-done(((f32[2048,128]{0,1:T(8,128)}), f32[2048,128]{0,1:T(8,128)}) %all-reduce.17.cloned.1.call-update) | async-done | bytes 1048592 | tf_op jit(solution)/shard_map/psum | solution.py:179
  664.0 2.5 copy.22
  (62 shorter events, 4.0 us)
Async XLA Ops:
  7.2 335.6 %copy-start = (bf16[512,2048]{1,0:T(8,128)(2,1)S(1)}, bf16[512,2048]{1,0:T(8,128)(2,1)}, u32[]{:S(2)}) copy-start(bf16[512,2048]{1,0:T(8,128)(2,1)} %param.22) | copy-start | bytes 6291460
  7.2 6.8 %copy-start.13 = (s32[8]{0:T(128)S(1)}, s32[8]{0:T(128)}, u32[]{:S(2)}) copy-start(s32[8]{0:T(128)} %param.17) | copy-start | bytes 100
  7.2 179.4 %all-reduce.9.cloned.1.call-start = ((), (), s32[]{:S(2)}) async-start(), calls=%async_computation | async-start | bytes 262144 | tf_op jit(solution)/shard_map/psum | solution.py:170
  19.5 6.7 copy-start.2
  26.2 5.2 copy-start.14
  32.7 154.6 %copy-start.8 = (f32[512]{0:T(512)S(1)}, f32[512]{0:T(512)}, u32[]{:S(2)}) copy-start(f32[512]{0:T(512)} %param.23) | copy-start | bytes 6148
  32.7 154.6 %copy-start.11 = (f32[512]{0:T(512)S(1)}, f32[512]{0:T(512)}, u32[]{:S(2)}) copy-start(f32[512]{0:T(512)} %param.24) | copy-start | bytes 6148
  41.2 300.9 %all-reduce.11.cloned.1.call-start = ((), (), s32[]{:S(2)}) async-start(), calls=%async_computation.1 | async-start | bytes 262144 | tf_op jit(solution)/shard_map/psum | solution.py:170
  187.3 8.1 %slice-start = ((s8[4718592]{0:T(1024)(128)(4,1)}), s8[4194304]{0:T(1024)(128)(4,1)S(1)}, s32[]{:S(2)}) async-start(s8[4718592]{0:T(1024)(128)(4,1)} %bitcast.147), calls=%async_computation.5 | async-start | bytes 8388608
  190.1 5.3 slice-start.1
  202.4 140.4 %copy-start.9 = (f32[512]{0:T(512)S(1)}, f32[512]{0:T(512)}, u32[]{:S(2)}) copy-start(f32[512]{0:T(512)} %param.25) | copy-start | bytes 6148
  202.4 140.4 %copy-start.12 = (f32[512]{0:T(512)S(1)}, f32[512]{0:T(512)}, u32[]{:S(2)}) copy-start(f32[512]{0:T(512)} %param.26) | copy-start | bytes 6148
  202.4 293.6 %all-reduce.13.cloned.1.call-start = ((), (), s32[]{:S(2)}) async-start(), calls=%async_computation.2 | async-start | bytes 1048576 | tf_op jit(solution)/shard_map/psum | solution.py:170
  342.8 9.2 %copy-start.3 = (bf16[2048,128]{1,0:T(8,128)(2,1)S(1)}, bf16[2048,128]{1,0:T(8,128)(2,1)}, u32[]{:S(2)}) copy-start(bf16[2048,128]{1,0:T(8,128)(2,1)} %param.30) | copy-start | bytes 1572868
  342.8 9.2 %copy-start.5 = (bf16[8,2048]{1,0:T(8,128)(2,1)S(1)}, bf16[8,2048]{1,0:T(8,128)(2,1)}, u32[]{:S(2)}) copy-start(bf16[8,2048]{1,0:T(8,128)(2,1)} %param.19) | copy-start | bytes 98308
  342.9 154.0 %copy-start.6 = (f32[2048]{0:T(1024)S(1)}, f32[2048]{0:T(1024)}, u32[]{:S(2)}) copy-start(f32[2048]{0:T(1024)} %param.27) | copy-start | bytes 24580
  342.9 154.0 %copy-start.7 = (f32[2048]{0:T(1024)S(1)}, f32[2048]{0:T(1024)}, u32[]{:S(2)}) copy-start(f32[2048]{0:T(1024)} %param.28) | copy-start | bytes 24580
  351.9 200.6 %all-reduce.15.cloned.1.call-start = ((), (), s32[]{:S(2)}) async-start(), calls=%async_computation.3 | async-start | bytes 2097152 | tf_op jit(solution)/shard_map/psum | solution.py:179
  496.9 5.9 copy-start.4
  496.9 6.2 copy-start.1
  505.8 2.5 copy-start.10
  509.7 154.3 %all-reduce.17.cloned.1.call-start = ((), (), s32[]{:S(2)}) async-start(), calls=%async_computation.4 | async-start | bytes 2097152 | tf_op jit(solution)/shard_map/psum | solution.py:179
Sparse Core Ops, SparseCore 0:
  41.3 145.2 all-reduce.8
  202.5 139.4 all-reduce.10
  352.1 143.9 all-reduce.12
  509.8 42.6 all-reduce.14
  555.6 108.3 all-reduce.16
